TPU v7x, 32 devices: a whole 2x2x4 slice. The times are simulated.
32 devices in a mesh: scen: 4 (over z), slab: 2 (over x), grp: 4 (over y, core).
Axes of the slice: x: 2, y: 2, z: 4, core: 2. Of those that a mesh axis runs over, the one named last changes fastest.
Arguments:
- factor_inverse: bfloat16 [4, 1536, 1536], P('grp', ('scen', 'slab')), may hold values from -0.102062073 to 2, as said below
- border_window: bfloat16 [4, 1536, 2048], P('grp', None, ('scen', 'slab')), may hold values from -0.47851562 to 0.47851562
- border_panel: bfloat16 [4, 1536, 1024], P('grp', None, 'slab'), may hold values from -0.47851562 to 0.47851562
- border_pattern: int32 [4, 16], P('grp', ('scen', 'slab')), may hold values 0 or 1
- earlier_rows: bfloat16 [4096, 2048], P('grp', ('scen', 'slab')), may hold values from -0.75 to 0.75
- earlier_panel: bfloat16 [4096, 1024], P('grp'), may hold values from -0.75 to 0.75
- pivot_inverse: bfloat16 [1024, 1024], P('grp'), may hold values from -0.125 to 2, as said below
Outputs:
- panel_factor: bfloat16 [1024, 2048], P('grp', ('scen', 'slab'))
Inputs may be any that keep to these rules, and one draw needn't show every extreme that they name: factor_inverse[s, k, i] is zero where i < k; its diagonal lies between 0.5 and 2. pivot_inverse[j, k] is zero where k > j; its diagonal lies between 0.5 and 2.
All inputs are finite; a program needn't handle non-finite values. No bound on the sum of `border_pattern` on one device may be relied on, other than what follows from the above.
Results may differ from a plain program's by a relative error of at most 0.0056.
Values may be sent and summed in bfloat16 or wider, within the bound.
A program may use at most 64 MiB of HBM per device.

v0:
```python
import jax
import jax.numpy as jnp
from jax import lax
from jax.sharding import PartitionSpec as P


def body(
    factor_inverse,
    border_window,
    border_panel,
    border_pattern,
    earlier_rows,
    earlier_panel,
    pivot_inverse,
):
    window = border_window[0]
    columns = window.shape[1]
    blocks = border_pattern.shape[1]
    column_mask = jnp.repeat(border_pattern[0].astype(jnp.bfloat16), columns // blocks)
    masked = window * column_mask[None, :]
    panel_border = border_panel[0]
    incoming = lax.all_gather(factor_inverse[0], ("scen", "slab"), axis=0, tiled=True)
    window_sum = lax.dot_general(
        incoming, masked, (((0,), (0,)), ((), ())), preferred_element_type=jnp.float32
    )
    panel_sum = lax.dot_general(
        panel_border, incoming, (((0,), (0,)), ((), ())), preferred_element_type=jnp.float32
    )
    window_sum, panel_sum = (window_sum, panel_sum)
    window_image = window_sum.astype(jnp.bfloat16)
    panel_piece = panel_sum.astype(jnp.bfloat16)
    panel_image = lax.all_gather(panel_piece, "slab", axis=0, tiled=True)
    contribution = jnp.dot(panel_image, window_image, preferred_element_type=jnp.float32)
    update = lax.dot_general(
        earlier_panel, earlier_rows, (((0,), (0,)), ((), ())), preferred_element_type=jnp.float32
    )
    partial_sum = contribution - update
    schur_block = lax.psum(partial_sum, "grp").astype(jnp.bfloat16)
    return jnp.dot(pivot_inverse, schur_block, preferred_element_type=jnp.float32).astype(
        jnp.bfloat16
    )


def solution(mesh):
    placed = (
        P("grp", ("scen", "slab"), None),
        P("grp", None, ("scen", "slab")),
        P("grp", None, "slab"),
        P("grp", ("scen", "slab")),
        P("grp", ("scen", "slab")),
        P("grp", None),
        P("grp", None),
    )
    return jax.shard_map(
        body, mesh=mesh, in_specs=placed, out_specs=P("grp", ("scen", "slab")), check_vma=False
    )
```

profile of v0, /device:TPU:29, one launch (start us, length us, event | category | flops | bytes accessed | tf_op | source)
XLA Modules:
  0.0 184.5 jit_solution(15503448348941178299)
XLA Ops:
  6.5 0.0 copy-start
  6.5 0.0 all-gather.6.cloned.1.call-start
  6.5 0.7 all-gather.6.cloned.1.call-update
  7.3 0.0 copy-start.4
  7.3 0.0 copy-start.2
  7.3 0.0 all-gather.4.cloned.1.call-start
  7.3 80.8 %all-gather.6.cloned.1.call-done = bf16[1,1536,1536]{2,1,0:T(8,128)(2,1)} async-done(((bf16[1,192,1536]{2,1,0:T(8,128)(2,1)}), bf16[1,1536,1536]{2,1,0:T(8,128)(2,1)}) %all-gather.6.cloned.1.call-update) | async-done | bytes 4718608 | tf_op jit(solution)/shard_map/all_gather | solution.py:22
  88.2 6.7 %fusion.4 = bf16[512,1536]{1,0:T(8,128)(2,1)} fusion(bf16[1,1536,1536]{2,1,0:T(8,128)(2,1)} %all-gather.6.cloned.1.call-done, bf16[1,1536,512]{2,1,0:T(8,128)(2,1)} %param.9), kind=kOutput, calls=%fused_computation.4 | convolution fusion | flops 2416705536 | bytes 7864320 | tf_op jit(solution)/shard_map/dot_general | solution.py:26
  94.9 0.0 all-gather.4.cloned.1.call-update
  94.9 0.0 copy-done.4
  94.9 0.1 broadcast_bitcast_fusion
  95.0 0.0 copy-start.3
  95.0 44.8 %all-gather.4.cloned.1.call-done = bf16[1024,1536]{1,0:T(8,128)(2,1)} async-done(((bf16[512,1536]{1,0:T(8,128)(2,1)}), bf16[1024,1536]{1,0:T(8,128)(2,1)}) %all-gather.4.cloned.1.call-update) | async-done | bytes 3145744 | tf_op jit(solution)/shard_map/all_gather | solution.py:32
  139.8 0.0 copy-done.2
  139.8 6.6 %fusion.13 = f32[1024,256]{1,0:T(8,128)} fusion(bf16[1024,1536]{1,0:T(8,128)(2,1)} %all-gather.4.cloned.1.call-done, bf16[1,1536,1536]{2,1,0:T(8,128)(2,1)} %all-gather.6.cloned.1.call-done, bf16[1,1536,256]{2,1,0:T(8,128)(2,1)S(1)} %copy-done.2, bf16[256]{0:T(256)(128)(2,1)S(1)} %broadcast_bitcast_fusion), kind=kOutput, calls=%fused_computation.11 | convolution fusion | flops 2014052352 | bytes 9699840 | tf_op jit(solution)/shard_map/dot_general | solution.py:33
  146.4 0.0 copy-done
  146.4 0.0 copy-done.3
  146.4 0.0 copy-start.1
  146.4 3.1 %convolution_subtract_fusion = f32[1024,256]{1,0:T(8,128)} fusion(f32[1024,256]{1,0:T(8,128)} %fusion.13, bf16[1024,1024]{1,0:T(8,128)(2,1)S(1)} %copy-done, bf16[1024,256]{1,0:T(8,128)(2,1)S(1)} %copy-done.3), kind=kOutput, calls=%fused_computation.7 | convolution fusion | flops 537133056 | bytes 4718592 | tf_op jit(solution)/shard_map/dot_general | solution.py:34
  149.5 26.9 %all-reduce.1 = bf16[1024,256]{1,0:T(8,128)(2,1)S(1)} all-reduce(f32[1024,256]{1,0:T(8,128)} %convolution_subtract_fusion), channel_id=1, replica_groups=mesh['scen'=4,'slab'=2,'grp'=4] {'grp'}, use_global_device_ids=true, to_apply=%region_0.0 | all-reduce | flops 262144 | bytes 1572864 | tf_op jit(solution)/shard_map/psum | solution.py:38
  176.5 0.0 copy-done.1
  176.5 0.3 fusion.11
  176.9 0.8 copy.8
  (1 shorter events, 0.0 us)
Async XLA Ops:
  6.5 139.9 %copy-start = (bf16[1024,1024]{1,0:T(8,128)(2,1)S(1)}, bf16[1024,1024]{1,0:T(8,128)(2,1)}, u32[]{:S(2)}) copy-start(bf16[1024,1024]{1,0:T(8,128)(2,1)} %param.12) | copy-start | bytes 6291460
  6.5 81.6 %all-gather.6.cloned.1.call-start = ((), (), s32[]{:S(2)}) async-start(), calls=%async_computation.1 | async-start | bytes 5308416 | tf_op jit(solution)/shard_map/all_gather | solution.py:22
  7.3 87.6 %copy-start.4 = (s32[1,2]{1,0:T(1,128)S(1)}, s32[1,2]{1,0:T(1,128)}, u32[]{:S(2)}) copy-start(s32[1,2]{1,0:T(1,128)} %param.10) | copy-start | bytes 28
  7.3 132.5 %copy-start.2 = (bf16[1,1536,256]{2,1,0:T(8,128)(2,1)S(1)}, bf16[1,1536,256]{2,1,0:T(8,128)(2,1)}, u32[]{:S(2)}) copy-start(bf16[1,1536,256]{2,1,0:T(8,128)(2,1)} %param.8) | copy-start | bytes 2359300
  7.3 132.5 %all-gather.4.cloned.1.call-start = ((), (), s32[]{:S(2)}) async-start(), calls=%async_computation | async-start | bytes 4718592 | tf_op jit(solution)/shard_map/all_gather | solution.py:32
  95.0 51.5 %copy-start.3 = (bf16[1024,256]{1,0:T(8,128)(2,1)S(1)}, bf16[1024,256]{1,0:T(8,128)(2,1)}, u32[]{:S(2)}) copy-start(bf16[1024,256]{1,0:T(8,128)(2,1)} %param.11) | copy-start | bytes 1572868
  146.4 30.1 %copy-start.1 = (bf16[256,1024]{1,0:T(8,128)(2,1)S(1)}, bf16[256,1024]{1,0:T(8,128)(2,1)}, u32[]{:S(2)}) copy-start(bf16[256,1024]{1,0:T(8,128)(2,1)} %param.13) | copy-start | bytes 1572868
Sparse Core Ops, SparseCore 0:
  9.5 78.5 all-gather.5
  95.0 44.7 all-gather.3
where the time goes:
time: 186 us; the launch traced here: 184 us
  waiting for transfers between devices  126 us (68%)
  blocking collectives  26.9 us (14%)
  matrix products  16.8 us (9%)
  between operations  13.5 us (7%)
    all_gather x1, waiting for transfers between devices, body(): lax.all_gather(factor_inverse[0], ('scen', 'slab'), axis=0, tiled=True)  80.8 us
    all_gather x1, waiting for transfers between devices, body(): panel_image = lax.all_gather(panel_piece, 'slab', axis=0, tiled=True)  44.8 us
    psum x1, blocking collectives, body(): schur_block = lax.psum(partial_sum, 'grp').astype(jnp.bfloat16)  26.9 us
    dot_general x1, matrix products, body(): lax.dot_general(panel_border, incoming, (((0,), (0,)), ((), ())), preferr...  6.7 us
    dot_general x1, matrix products, body(): jnp.dot(panel_image, window_image, preferred_element_type=jnp.float32)  6.65 us
  transfers between devices with their start and end apart: 2, of which 2 were waited for; matrix products, arithmetic and copies ran while one was open for 0% of the time, Pallas kernels for 0%

commit v1 on v0

--- a/solution.py
+++ b/solution.py
@@ -1,7 +1,489 @@
+import functools
+
 import jax
 import jax.numpy as jnp
 from jax import lax
+from jax.experimental import pallas as pl
+from jax.experimental.pallas import tpu as pltpu
 from jax.sharding import PartitionSpec as P
+
+
+F32 = jnp.float32
+BF16 = jnp.bfloat16
+MESH = pl.DeviceIdType.MESH
+
+
+def event_codes(nz):
+    codes = []
+    for z in range(nz):
+        pairs = sorted(range(nz), key=lambda p: (abs(p - z), p < z))
+        events = [(p, j) for p in pairs for j in range(p, nz)]
+        codes.append(
+            (
+                sum(p * nz**e for e, (p, j) in enumerate(events)),
+                sum(j * nz**e for e, (p, j) in enumerate(events)),
+            )
+        )
+    return codes
+
+
+def pick(index, values):
+    chosen = jnp.int32(values[0])
+    for i, value in enumerate(values[1:], 1):
+        chosen = jnp.where(index == i, jnp.int32(value), chosen)
+    return chosen
+
+
+def panel_kernel(
+    nz,
+    f_in,
+    bw_in,
+    bp_in,
+    pat,
+    er_in,
+    ep_in,
+    pv_in,
+    out,
+    fg,
+    bw,
+    bp,
+    er,
+    ep,
+    pv,
+    bt,
+    acc,
+    tot,
+    half,
+    ybuf,
+    yrecv,
+    sch,
+    loc_sem,
+    f_recv,
+    up_sem,
+    dn_sem,
+    xs_sem,
+    bp_send,
+    bp_recv,
+    c_send,
+    c_recv,
+    y_send,
+    y_recv,
+    s_send,
+    s_fwd,
+    s_recv,
+):
+    z = lax.axis_index("scen")
+    x = lax.axis_index("slab")
+    g = lax.axis_index("grp")
+    ox = 1 - x
+    core = g + 1 - 2 * lax.rem(g, 2)
+    far = lax.rem(g + 2, 4)
+    last = nz - 1
+    rows = f_in.shape[1]
+    order = f_in.shape[2]
+    wide = order // nz
+    pc = bp_in.shape[2]
+    wc = bw_in.shape[2]
+    count = nz * (nz + 1) // 2
+    codes = event_codes(nz)
+    code_p = pick(z, [c[0] for c in codes])
+    code_j = pick(z, [c[1] for c in codes])
+    up_id, dn_id, x_id = {"scen": z + 1}, {"scen": z - 1}, {"slab": ox}
+
+    own = 2 * z + x
+    locals_ = [
+        pltpu.make_async_copy(f_in.at[0], fg.at[own], loc_sem.at[0]),
+        pltpu.make_async_copy(bw_in.at[0], bw, loc_sem.at[1]),
+        pltpu.make_async_copy(bp_in.at[0], bp.at[x], loc_sem.at[2]),
+        pltpu.make_async_copy(er_in, er, loc_sem.at[3]),
+        pltpu.make_async_copy(ep_in, ep, loc_sem.at[4]),
+        pltpu.make_async_copy(pv_in, pv, loc_sem.at[5]),
+    ]
+    for c in locals_:
+        c.start()
+
+    barrier = pltpu.get_barrier_semaphore()
+
+    @pl.when(z < last)
+    def _():
+        pl.semaphore_signal(barrier, inc=1, device_id=up_id, device_id_type=MESH)
+
+    @pl.when(z > 0)
+    def _():
+        pl.semaphore_signal(barrier, inc=1, device_id=dn_id, device_id_type=MESH)
+
+    for peer in (x_id, {"grp": core}, {"grp": far}):
+        pl.semaphore_signal(barrier, inc=1, device_id=peer, device_id_type=MESH)
+    pl.semaphore_wait(barrier, 3 + jnp.where(z < last, 1, 0) + jnp.where(z > 0, 1, 0))
+
+    def cols(j):
+        return pl.ds(pl.multiple_of(j * wide, 128), wide)
+
+    def piece(d, j, sems, peer, src=None):
+        here = fg.at[d, :, cols(j)]
+        return pltpu.make_async_remote_copy(
+            src_ref=here if src is None else src,
+            dst_ref=here,
+            send_sem=sems.at[d, j],
+            recv_sem=f_recv.at[d, j],
+            device_id=peer,
+            device_id_type=MESH,
+        )
+
+    def goes_up(p, b, j):
+        single = (z == last - 1) & (p == 0) & (j >= 1) & (b != x)
+        return (z < last) & (p <= z) & jnp.logical_not(single)
+
+    def goes_x(p, b, j):
+        return (z == last) & (p == 0) & (j >= 1) & (b == x)
+
+    def send_own(j, carry):
+        src = f_in.at[0, :, cols(j)]
+        piece(own, j, xs_sem, x_id, src).start()
+
+        @pl.when(z < last)
+        def _():
+            piece(own, j, up_sem, up_id, src).start()
+
+        @pl.when(z > 0)
+        def _():
+            piece(own, j, dn_sem, dn_id, src).start()
+
+        return carry
+
+    lax.fori_loop(z, nz, send_own, 0)
+
+    def krows(p):
+        return pl.ds(pl.multiple_of(p * wide, 128), wide)
+
+    def panel_chunk(p):
+        return pltpu.make_async_remote_copy(
+            src_ref=bp_in.at[0, krows(p), :],
+            dst_ref=bp.at[x, krows(p), :],
+            send_sem=bp_send.at[p],
+            recv_sem=bp_recv.at[p],
+            device_id=x_id,
+            device_id_type=MESH,
+        )
+
+    def send_panel(e, carry):
+        cp, cj = carry
+        p, j = lax.rem(cp, nz), lax.rem(cj, nz)
+
+        @pl.when(p == j)
+        def _():
+            panel_chunk(p).start()
+
+        return cp // nz, cj // nz
+
+    lax.fori_loop(0, count, send_panel, (code_p, code_j))
+
+    acc[...] = jnp.zeros_like(acc)
+
+    locals_[2].wait()
+    locals_[1].wait()
+    blocks = pat.shape[1]
+    lane = wc // blocks
+
+    @pl.loop(0, nz)
+    def _(p):
+        for t in range(pc // 256):
+            r = pl.ds(pl.multiple_of(x * pc + t * 256, 128), 256)
+            bt[r, cols(p)] = bp[x, krows(p), t * 256 : (t + 1) * 256].T
+        for t in range(blocks):
+            r = pl.ds(2 * pc + t * lane, lane)
+            m = pat[0, t].astype(F32).astype(BF16)
+            bt[r, cols(p)] = bw[krows(p), t * lane : (t + 1) * lane].T * m
+
+    locals_[3].wait()
+    locals_[4].wait()
+    quarter = tot.shape[1]
+
+    @pl.loop(0, 4)
+    def _(q):
+        c = pl.ds(pl.multiple_of(q * quarter, 128), quarter)
+        tot[q] = -lax.dot_general(
+            ep[:, c], er[...], (((0,), (0,)), ((), ())), preferred_element_type=F32
+        )
+
+    locals_[0].wait()
+    locals_[5].wait()
+
+    def accumulate(p, j, first, tiles):
+        low = fg[2 * p, :, cols(j)]
+        high = fg[2 * p + 1, :, cols(j)]
+        right = jnp.concatenate([low, high], axis=0)
+        for t in range(tiles):
+            r = pl.ds(pl.multiple_of(first + t * 256, 128), 256)
+            acc[r, cols(j)] += jnp.dot(bt[r, cols(p)], right, preferred_element_type=F32)
+
+    def pass_on(p, b, j):
+        d = 2 * p + b
+
+        @pl.when((p != z) | (b != x))
+        def _():
+            piece(d, j, up_sem, up_id).wait_recv()
+
+            @pl.when(goes_up(p, b, j))
+            def _():
+                piece(d, j, up_sem, up_id).start()
+
+            @pl.when((z > 0) & (p >= z))
+            def _():
+                piece(d, j, dn_sem, dn_id).start()
+
+            @pl.when(goes_x(p, b, j))
+            def _():
+                piece(d, j, xs_sem, x_id).start()
+
+    lag = min(4, count - 1)
+
+    def partner(p, j):
+        @pl.when(p == j)
+        def _():
+            panel_chunk(p).wait_recv()
+            for t in range(pc // 256):
+                r = pl.ds(pl.multiple_of(ox * pc + t * 256, 128), 256)
+                bt[r, cols(p)] = bp[ox, krows(p), t * 256 : (t + 1) * 256].T
+
+        accumulate(p, j, ox * pc, pc // 256)
+
+    def digits(cp, cj):
+        return lax.rem(cp, nz), lax.rem(cj, nz)
+
+    pass_on(*[v for v in (lax.rem(code_p, nz), x, lax.rem(code_j, nz))])
+
+    def event(e, carry):
+        cp, cj, lp, lj = carry
+        p, j = digits(cp, cj)
+        np_, nj = cp // nz, cj // nz
+
+        @pl.when(e < count - 1)
+        def _():
+            a, b = digits(np_, nj)
+            pass_on(a, x, b)
+
+        pass_on(p, ox, j)
+        accumulate(p, j, x * pc, pc // 256)
+        accumulate(p, j, 2 * pc, wc // 256)
+        late = e >= lag
+        a, b = digits(lp, lj)
+
+        @pl.when(late)
+        def _():
+            partner(a, b)
+
+        return np_, nj, jnp.where(late, lp // nz, lp), jnp.where(late, lj // nz, lj)
+
+    _, _, lp, lj = lax.fori_loop(0, count, event, (code_p, code_j, code_p, code_j))
+
+    def rest(e, carry):
+        lp, lj = carry
+        a, b = digits(lp, lj)
+        partner(a, b)
+        return lp // nz, lj // nz
+
+    lax.fori_loop(0, lag, rest, (lp, lj))
+
+    window = acc[2 * pc : 2 * pc + wc, :].astype(BF16)
+
+    def share(q):
+        r = pl.ds(pl.multiple_of(q * quarter, 128), quarter)
+        tot[q] += lax.dot_general(
+            acc[r, :].astype(BF16), window, (((1,), (1,)), ((), ())), preferred_element_type=F32
+        )
+
+    def to_core(q, slot):
+        return pltpu.make_async_remote_copy(
+            src_ref=tot.at[q],
+            dst_ref=half.at[slot],
+            send_sem=c_send.at[slot],
+            recv_sem=c_recv.at[slot],
+            device_id={"grp": core},
+            device_id_type=MESH,
+        )
+
+    first, second = to_core(3 - g, 0), to_core(core, 1)
+    share(3 - g)
+    first.start()
+    share(core)
+    second.start()
+    share(far)
+    first.wait_recv()
+    ybuf[...] = (tot[far] + half[0]).astype(BF16)
+    across = pltpu.make_async_remote_copy(
+        src_ref=ybuf,
+        dst_ref=yrecv,
+        send_sem=y_send,
+        recv_sem=y_recv,
+        device_id={"grp": far},
+        device_id_type=MESH,
+    )
+    across.start()
+    share(g)
+    second.wait_recv()
+    mine = tot[g] + half[1]
+    across.wait_recv()
+    sch[g] = (mine + yrecv[...].astype(F32)).astype(BF16)
+
+    def give(q, sems, slot, to):
+        return pltpu.make_async_remote_copy(
+            src_ref=sch.at[q],
+            dst_ref=sch.at[q],
+            send_sem=sems.at[slot],
+            recv_sem=s_recv.at[q],
+            device_id={"grp": to},
+            device_id_type=MESH,
+        )
+
+    @pl.when(g < 2)
+    def _():
+        give(g, s_send, 0, far).start()
+
+    @pl.when(lax.rem(g, 2) == 0)
+    def _():
+        give(g, s_send, 1, core).start()
+
+    @pl.when(g >= 2)
+    def _():
+        give(far, s_fwd, 0, core).wait_recv()
+        give(far, s_fwd, 0, core).start()
+
+    def part(q):
+        c = pl.ds(pl.multiple_of(q * quarter, 128), quarter)
+        return jnp.dot(pv[:, c], sch[q], preferred_element_type=F32)
+
+    res = half.at[0]
+    res[...] = part(g)
+
+    @pl.when(g >= 2)
+    def _():
+        res[...] += part(far)
+
+    @pl.when(lax.rem(g, 2) == 1)
+    def _():
+        give(core, s_fwd, 0, core).wait_recv()
+        res[...] += part(core)
+
+    @pl.when(g >= 2)
+    def _():
+        give(3 - g, s_fwd, 0, core).wait_recv()
+        res[...] += part(3 - g)
+
+    out[...] = res[...].astype(out.dtype)
+
+    first.wait_send()
+    second.wait_send()
+    across.wait_send()
+
+    @pl.when(g < 2)
+    def _():
+        give(g, s_send, 0, far).wait_send()
+
+    @pl.when(lax.rem(g, 2) == 0)
+    def _():
+        give(g, s_send, 1, core).wait_send()
+
+    @pl.when(g >= 2)
+    def _():
+        give(far, s_fwd, 0, core).wait_send()
+
+    def drain(e, carry):
+        cp, cj = carry
+        p, j = digits(cp, cj)
+
+        @pl.when(p == j)
+        def _():
+            panel_chunk(p).wait_send()
+
+        for b in range(2):
+            d = 2 * p + b
+
+            @pl.when(goes_up(p, b, j))
+            def _():
+                piece(d, j, up_sem, up_id).wait_send()
+
+            @pl.when((z > 0) & (p >= z))
+            def _():
+                piece(d, j, dn_sem, dn_id).wait_send()
+
+            @pl.when(goes_x(p, b, j) | ((p == z) & (b == x)))
+            def _():
+                piece(d, j, xs_sem, x_id).wait_send()
+
+        return cp // nz, cj // nz
+
+    lax.fori_loop(0, count, drain, (code_p, code_j))
+
+
+def fused(nz):
+    def run(f, bw, bp, pat, er, ep, pv):
+        rows, order = f.shape[1:]
+        pc, wc, total = bp.shape[2], bw.shape[2], ep.shape[1]
+        dma = pltpu.SemaphoreType.DMA
+        anywhere = pl.BlockSpec(memory_space=pl.ANY)
+        return pl.pallas_call(
+            functools.partial(panel_kernel, nz),
+            out_shape=jax.ShapeDtypeStruct((pv.shape[0], wc), BF16),
+            in_specs=[anywhere] * 3
+            + [pl.BlockSpec(memory_space=pltpu.SMEM)]
+            + [anywhere] * 3,
+            out_specs=pl.BlockSpec(memory_space=pltpu.VMEM),
+            scratch_shapes=[
+                pltpu.VMEM((2 * nz, rows, order), BF16),
+                pltpu.VMEM((order, wc), BF16),
+                pltpu.VMEM((2, order, pc), BF16),
+                pltpu.VMEM(er.shape, BF16),
+                pltpu.VMEM(ep.shape, BF16),
+                pltpu.VMEM(pv.shape, BF16),
+                pltpu.VMEM((2 * pc + wc, order), BF16),
+                pltpu.VMEM((2 * pc + wc, order), F32),
+                pltpu.VMEM((4, total // 4, wc), F32),
+                pltpu.VMEM((2, total // 4, wc), F32),
+                pltpu.VMEM((total // 4, wc), BF16),
+                pltpu.VMEM((total // 4, wc), BF16),
+                pltpu.VMEM((4, total // 4, wc), BF16),
+                dma((6,)),
+                dma((2 * nz, nz)),
+                dma((2 * nz, nz)),
+                dma((2 * nz, nz)),
+                dma((2 * nz, nz)),
+                dma((nz,)),
+                dma((nz,)),
+                dma((2,)),
+                dma((2,)),
+                dma,
+                dma,
+                dma((2,)),
+                dma((1,)),
+                dma((4,)),
+            ],
+            compiler_params=pltpu.CompilerParams(
+                collective_id=0, has_side_effects=True, vmem_limit_bytes=60 * 2**20
+            ),
+        )(f, bw, bp, pat, er, ep, pv)
+
+    return run
+
+
+def fits(mesh, f, bw, bp, pat, er, ep, pv):
+    nz = mesh.shape["scen"]
+    order = f.shape[2]
+    return (
+        mesh.shape["slab"] == 2
+        and mesh.shape["grp"] == 4
+        and nz >= 2
+        and order % (128 * nz) == 0
+        and f.shape[1] * 2 * nz == order
+        and f.shape[1] % 16 == 0
+        and bw.shape[2] % 256 == 0
+        and bp.shape[2] % 256 == 0
+        and ep.shape[1] == 2 * bp.shape[2]
+        and ep.shape[1] % 512 == 0
+        and pv.shape[0] * 4 == ep.shape[1]
+        and (bw.shape[2] // pat.shape[1]) % 128 == 0
+        and nz ** (nz * (nz + 1) // 2) < 2**31
+    )
 
 
 def body(
@@ -51,6 +533,12 @@
         P("grp", None),
         P("grp", None),
     )
+
+    def either(*blocks):
+        if fits(mesh, *blocks):
+            return fused(mesh.shape["scen"])(*blocks)
+        return body(*blocks)
+
     return jax.shard_map(
-        body, mesh=mesh, in_specs=placed, out_specs=P("grp", ("scen", "slab")), check_vma=False
-    )
+        either, mesh=mesh, in_specs=placed, out_specs=P("grp", ("scen", "slab")), check_vma=False
+    )

time: 186 us -> 76.5 us (0.41)
  waiting for transfers between devices: 126 us -> 0 us
  Pallas kernels: 0 us -> 74.8 us
  blocking collectives: 26.9 us -> 0 us
  matrix products: 16.8 us -> 0 us
  between operations: 13.5 us -> 0.01 us
    all_gather x2 -> x0, waiting for transfers between devices: 126 us -> none  [the longest x1 80.8 us: body(): lax.all_gather(factor_inverse[0], ('scen', 'slab'), axis=0, tiled=True)]
    pallas_call x0 -> x1, Pallas kernels: none -> 74.8 us  [run(): pl.pallas_call(functools.partial(panel_kernel, nz), out_shape=jax.ShapeDt...]
    psum x1 -> x0, blocking collectives: 26.9 us -> none  [body(): schur_block = lax.psum(partial_sum, 'grp').astype(jnp.bfloat16)]
    dot_general x4 -> x0, matrix products: 16.8 us -> none  [the longest x1 6.7 us: body(): lax.dot_general(panel_border, incoming, (((0,), (0,)), ((), ())), preferr...]
  transfers between devices with their start and end apart: 2 -> 0, of which waited for: 2 -> 0; matrix products, arithmetic and copies ran while one was open for 0% -> 0% of each run, Pallas kernels for 0% -> 0%
where the time goes in v1:
time: 76.5 us; the launch traced here: 76.4 us
  Pallas kernels  74.8 us (98%)
  local copies, waits for them, and re-layouts  1.57 us (2%)
    pallas_call x1, Pallas kernels, run(): pl.pallas_call(functools.partial(panel_kernel, nz), out_shape=jax.ShapeDt...  74.8 us
    unnamed x1, local copies, waits for them, and re-layouts  1.57 us

profile of v1, /device:TPU:29, one launch (start us, length us, event | category | flops | bytes accessed | tf_op | source)
XLA Modules:
  0.0 76.4 jit_solution(10499637835180584000)
XLA Ops:
  0.0 74.8 %shard_map.73 = bf16[256,256]{1,0:T(8,128)(2,1)} custom-call(bf16[1,192,1536]{2,1,0:T(8,128)(2,1)} %f_in.1, bf16[1,1536,256]{2,1,0:T(8,128)(2,1)} %bw_in.1, bf16[1,1536,512]{2,1,0:T(8,128)(2,1)} %bp_in.1, s32[1,2]{1,0:T(1,128)} %pat.1, bf16[1024,256]{1,0:T(8,128)(2,1)} %er_in.1, bf16[1024,1024]{1,0:T(8,128)(2,1)} %ep_in.1, bf16[256,1024]{1,0:T(8,128)(2,1)} %pv_in.1), custom_call_target="tpu_custom_call" | custom-call | tf_op jit(solution)/shard_map/pallas_call | solution.py:425
  74.8 1.6 %copy.9 = bf16[256,256]{1,0:T(8,128)(2,1)} copy(bf16[256,256]{1,0:T(8,128)(2,1)} %shard_map.73) | data formatting | bytes 262144

commit v2 on v1

--- a/solution.py
+++ b/solution.py
@@ -102,6 +102,13 @@
     for c in locals_:
         c.start()
 
+    cut = rows // 128 * 128
+    for p in range(nz if cut else 0):
+
+        @pl.when(z != p)
+        def _():
+            fg[2 * p + 1, :, p * wide : p * wide + cut] = jnp.zeros((rows, cut), BF16)
+
     barrier = pltpu.get_barrier_semaphore()
 
     @pl.when(z < last)
@@ -119,35 +126,52 @@
     def cols(j):
         return pl.ds(pl.multiple_of(j * wide, 128), wide)
 
-    def piece(d, j, sems, peer, src=None):
-        here = fg.at[d, :, cols(j)]
-        return pltpu.make_async_remote_copy(
-            src_ref=here if src is None else src,
-            dst_ref=here,
-            send_sem=sems.at[d, j],
-            recv_sem=f_recv.at[d, j],
-            device_id=peer,
-            device_id_type=MESH,
-        )
+    def piece(action, p, b, j, sems, peer, input_block=False):
+        d = 2 * p + b
+        short = (p == j) & (b == 1)
+
+        def copy(skip):
+            c = pl.ds(pl.multiple_of(j * wide + skip, 128), wide - skip)
+            here = fg.at[d, :, c]
+            getattr(
+                pltpu.make_async_remote_copy(
+                    src_ref=f_in.at[0, :, c] if input_block else here,
+                    dst_ref=here,
+                    send_sem=sems.at[d, j],
+                    recv_sem=f_recv.at[d, j],
+                    device_id=peer,
+                    device_id_type=MESH,
+                ),
+                action,
+            )()
+
+        @pl.when(short)
+        def _():
+            copy(cut)
+
+        @pl.when(jnp.logical_not(short))
+        def _():
+            copy(0)
+
+    def alone(to, p, j):
+        return (to == last) & (p == 0) & (j < last)
 
     def goes_up(p, b, j):
-        single = (z == last - 1) & (p == 0) & (j >= 1) & (b != x)
-        return (z < last) & (p <= z) & jnp.logical_not(single)
+        return (z < last) & (p <= z) & jnp.logical_not(alone(z + 1, p, j) & (b != x))
 
     def goes_x(p, b, j):
-        return (z == last) & (p == 0) & (j >= 1) & (b == x)
+        return alone(z, p, j) & (b == x)
 
     def send_own(j, carry):
-        src = f_in.at[0, :, cols(j)]
-        piece(own, j, xs_sem, x_id, src).start()
+        piece("start", z, x, j, xs_sem, x_id, True)
 
         @pl.when(z < last)
         def _():
-            piece(own, j, up_sem, up_id, src).start()
+            piece("start", z, x, j, up_sem, up_id, True)
 
         @pl.when(z > 0)
         def _():
-            piece(own, j, dn_sem, dn_id, src).start()
+            piece("start", z, x, j, dn_sem, dn_id, True)
 
         return carry
 
@@ -218,25 +242,21 @@
             acc[r, cols(j)] += jnp.dot(bt[r, cols(p)], right, preferred_element_type=F32)
 
     def pass_on(p, b, j):
-        d = 2 * p + b
-
         @pl.when((p != z) | (b != x))
         def _():
-            piece(d, j, up_sem, up_id).wait_recv()
+            piece("wait_recv", p, b, j, up_sem, up_id)
 
             @pl.when(goes_up(p, b, j))
             def _():
-                piece(d, j, up_sem, up_id).start()
+                piece("start", p, b, j, up_sem, up_id)
 
             @pl.when((z > 0) & (p >= z))
             def _():
-                piece(d, j, dn_sem, dn_id).start()
+                piece("start", p, b, j, dn_sem, dn_id)
 
             @pl.when(goes_x(p, b, j))
             def _():
-                piece(d, j, xs_sem, x_id).start()
-
-    lag = min(4, count - 1)
+                piece("start", p, b, j, xs_sem, x_id)
 
     def partner(p, j):
         @pl.when(p == j)
@@ -253,8 +273,17 @@
 
     pass_on(*[v for v in (lax.rem(code_p, nz), x, lax.rem(code_j, nz))])
 
+    def due(e):
+        behind = jnp.where((z == last) & (e >= count - nz), e, jnp.maximum(e - 3, 0))
+        return jnp.where(e == count - 1, count, behind)
+
+    def late(i, carry):
+        lp, lj = carry
+        partner(*digits(lp, lj))
+        return lp // nz, lj // nz
+
     def event(e, carry):
-        cp, cj, lp, lj = carry
+        cp, cj, done, lp, lj = carry
         p, j = digits(cp, cj)
         np_, nj = cp // nz, cj // nz
 
@@ -266,24 +295,11 @@
         pass_on(p, ox, j)
         accumulate(p, j, x * pc, pc // 256)
         accumulate(p, j, 2 * pc, wc // 256)
-        late = e >= lag
-        a, b = digits(lp, lj)
-
-        @pl.when(late)
-        def _():
-            partner(a, b)
-
-        return np_, nj, jnp.where(late, lp // nz, lp), jnp.where(late, lj // nz, lj)
-
-    _, _, lp, lj = lax.fori_loop(0, count, event, (code_p, code_j, code_p, code_j))
-
-    def rest(e, carry):
-        lp, lj = carry
-        a, b = digits(lp, lj)
-        partner(a, b)
-        return lp // nz, lj // nz
-
-    lax.fori_loop(0, lag, rest, (lp, lj))
+        target = due(e)
+        lp, lj = lax.fori_loop(done, target, late, (lp, lj))
+        return np_, nj, target, lp, lj
+
+    lax.fori_loop(0, count, event, (code_p, code_j, jnp.int32(0), code_p, code_j))
 
     window = acc[2 * pc : 2 * pc + wc, :].astype(BF16)
 
@@ -397,19 +413,17 @@
             panel_chunk(p).wait_send()
 
         for b in range(2):
-            d = 2 * p + b
-
             @pl.when(goes_up(p, b, j))
             def _():
-                piece(d, j, up_sem, up_id).wait_send()
+                piece("wait_send", p, b, j, up_sem, up_id)
 
             @pl.when((z > 0) & (p >= z))
             def _():
-                piece(d, j, dn_sem, dn_id).wait_send()
+                piece("wait_send", p, b, j, dn_sem, dn_id)
 
             @pl.when(goes_x(p, b, j) | ((p == z) & (b == x)))
             def _():
-                piece(d, j, xs_sem, x_id).wait_send()
+                piece("wait_send", p, b, j, xs_sem, x_id)
 
         return cp // nz, cj // nz
 

time: 76.5 us -> 71.2 us (0.931)
  Pallas kernels: 74.8 us -> 69.5 us
    pallas_call x1, Pallas kernels: 74.8 us -> 69.5 us  [run(): pl.pallas_call(functools.partial(panel_kernel, nz), out_shape=jax.ShapeDt...]
where the time goes in v2:
time: 71.2 us; the launch traced here: 71.1 us
  Pallas kernels  69.5 us (98%)
  local copies, waits for them, and re-layouts  1.57 us (2%)
    pallas_call x1, Pallas kernels, run(): pl.pallas_call(functools.partial(panel_kernel, nz), out_shape=jax.ShapeDt...  69.5 us
    unnamed x1, local copies, waits for them, and re-layouts  1.57 us

profile of v2, /device:TPU:29, one launch (start us, length us, event | category | flops | bytes accessed | tf_op | source)
XLA Modules:
  0.0 71.1 jit_solution(9637555471304352278)
XLA Ops:
  0.0 69.5 %shard_map.73 = bf16[256,256]{1,0:T(8,128)(2,1)} custom-call(bf16[1,192,1536]{2,1,0:T(8,128)(2,1)} %f_in.1, bf16[1,1536,256]{2,1,0:T(8,128)(2,1)} %bw_in.1, bf16[1,1536,512]{2,1,0:T(8,128)(2,1)} %bp_in.1, s32[1,2]{1,0:T(1,128)} %pat.1, bf16[1024,256]{1,0:T(8,128)(2,1)} %er_in.1, bf16[1024,1024]{1,0:T(8,128)(2,1)} %ep_in.1, bf16[256,1024]{1,0:T(8,128)(2,1)} %pv_in.1), custom_call_target="tpu_custom_call" | custom-call | tf_op jit(solution)/shard_map/pallas_call | solution.py:439
  69.5 1.6 %copy.9 = bf16[256,256]{1,0:T(8,128)(2,1)} copy(bf16[256,256]{1,0:T(8,128)(2,1)} %shard_map.73) | data formatting | bytes 262144

commit v3 on v2

--- a/solution.py
+++ b/solution.py
@@ -25,6 +25,19 @@
             )
         )
     return codes
+
+
+def diagonal_steps(rows):
+    steps = []
+    for b in range(2):
+        base = b * rows
+        skip = base // 128 * 128
+        edge = skip + 128 - base
+        if edge < rows and edge % 16 == 0:
+            steps.append([(0, edge, skip), (edge, rows - edge, skip + 128)])
+        else:
+            steps.append([(0, rows, skip)])
+    return steps
 
 
 def pick(index, values):
@@ -102,12 +115,16 @@
     for c in locals_:
         c.start()
 
-    cut = rows // 128 * 128
-    for p in range(nz if cut else 0):
+    steps = diagonal_steps(rows)
+    for p in range(nz):
 
         @pl.when(z != p)
         def _():
-            fg[2 * p + 1, :, p * wide : p * wide + cut] = jnp.zeros((rows, cut), BF16)
+            for b, parts in enumerate(steps):
+                for first, height, skip in parts:
+                    if skip:
+                        gap = fg.at[2 * p + b, first : first + height, p * wide : p * wide + skip]
+                        gap[...] = jnp.zeros(gap.shape, BF16)
 
     barrier = pltpu.get_barrier_semaphore()
 
@@ -128,33 +145,36 @@
 
     def piece(action, p, b, j, sems, peer, input_block=False):
         d = 2 * p + b
-        short = (p == j) & (b == 1)
-
-        def copy(skip):
+
+        def copy(index, first, height, skip):
             c = pl.ds(pl.multiple_of(j * wide + skip, 128), wide - skip)
-            here = fg.at[d, :, c]
+            r = pl.ds(first, height)
+            here = fg.at[d, r, c]
             getattr(
                 pltpu.make_async_remote_copy(
-                    src_ref=f_in.at[0, :, c] if input_block else here,
+                    src_ref=f_in.at[0, r, c] if input_block else here,
                     dst_ref=here,
-                    send_sem=sems.at[d, j],
-                    recv_sem=f_recv.at[d, j],
+                    send_sem=sems.at[d, j + index],
+                    recv_sem=f_recv.at[d, j + index],
                     device_id=peer,
                     device_id_type=MESH,
                 ),
                 action,
             )()
 
-        @pl.when(short)
-        def _():
-            copy(cut)
-
-        @pl.when(jnp.logical_not(short))
-        def _():
-            copy(0)
+        for half_block, parts in enumerate(steps):
+
+            @pl.when((p == j) & (b == half_block))
+            def _():
+                for index, part in enumerate(parts):
+                    copy(index * (nz - j), *part)
+
+        @pl.when(p != j)
+        def _():
+            copy(0, 0, rows, 0)
 
     def alone(to, p, j):
-        return (to == last) & (p == 0) & (j < last)
+        return (to == last) & (p == 0) & (2 * j < nz)
 
     def goes_up(p, b, j):
         return (z < last) & (p <= z) & jnp.logical_not(alone(z + 1, p, j) & (b != x))
@@ -309,61 +329,66 @@
             acc[r, :].astype(BF16), window, (((1,), (1,)), ((), ())), preferred_element_type=F32
         )
 
-    def to_core(q, slot):
+    def to_core(q, slot, r):
         return pltpu.make_async_remote_copy(
-            src_ref=tot.at[q],
-            dst_ref=half.at[slot],
+            src_ref=tot.at[q, r, :],
+            dst_ref=half.at[min(slot, 2) // 2, r, :],
             send_sem=c_send.at[slot],
             recv_sem=c_recv.at[slot],
             device_id={"grp": core},
             device_id_type=MESH,
         )
 
-    first, second = to_core(3 - g, 0), to_core(core, 1)
+    mid = quarter // 2
+    halves = [pl.ds(0, mid), pl.ds(mid, mid)]
+    first = [to_core(3 - g, h, r) for h, r in enumerate(halves)]
+    second = to_core(core, 2, pl.ds(0, quarter))
+    across = [
+        pltpu.make_async_remote_copy(
+            src_ref=ybuf.at[r, :],
+            dst_ref=yrecv.at[r, :],
+            send_sem=y_send.at[h],
+            recv_sem=y_recv.at[h],
+            device_id={"grp": far},
+            device_id_type=MESH,
+        )
+        for h, r in enumerate(halves)
+    ]
+
+    def give(q, h, sems, slot, to):
+        here = sch.at[q, halves[h], :]
+        return pltpu.make_async_remote_copy(
+            src_ref=here,
+            dst_ref=here,
+            send_sem=sems.at[slot, h],
+            recv_sem=s_recv.at[q, h],
+            device_id={"grp": to},
+            device_id_type=MESH,
+        )
+
     share(3 - g)
-    first.start()
+    for c in first:
+        c.start()
     share(core)
     second.start()
     share(far)
-    first.wait_recv()
-    ybuf[...] = (tot[far] + half[0]).astype(BF16)
-    across = pltpu.make_async_remote_copy(
-        src_ref=ybuf,
-        dst_ref=yrecv,
-        send_sem=y_send,
-        recv_sem=y_recv,
-        device_id={"grp": far},
-        device_id_type=MESH,
-    )
-    across.start()
+    for h, r in enumerate(halves):
+        first[h].wait_recv()
+        ybuf[r, :] = (tot[far, r, :] + half[0, r, :]).astype(BF16)
+        across[h].start()
     share(g)
     second.wait_recv()
-    mine = tot[g] + half[1]
-    across.wait_recv()
-    sch[g] = (mine + yrecv[...].astype(F32)).astype(BF16)
-
-    def give(q, sems, slot, to):
-        return pltpu.make_async_remote_copy(
-            src_ref=sch.at[q],
-            dst_ref=sch.at[q],
-            send_sem=sems.at[slot],
-            recv_sem=s_recv.at[q],
-            device_id={"grp": to},
-            device_id_type=MESH,
-        )
-
-    @pl.when(g < 2)
-    def _():
-        give(g, s_send, 0, far).start()
-
-    @pl.when(lax.rem(g, 2) == 0)
-    def _():
-        give(g, s_send, 1, core).start()
-
-    @pl.when(g >= 2)
-    def _():
-        give(far, s_fwd, 0, core).wait_recv()
-        give(far, s_fwd, 0, core).start()
+    for h, r in enumerate(halves):
+        across[h].wait_recv()
+        sch[g, r, :] = (tot[g, r, :] + half[1, r, :] + yrecv[r, :].astype(F32)).astype(BF16)
+
+        @pl.when(g < 2)
+        def _():
+            give(g, h, s_send, 0, far).start()
+
+        @pl.when(lax.rem(g, 2) == 0)
+        def _():
+            give(g, h, s_send, 1, core).start()
 
     def part(q):
         c = pl.ds(pl.multiple_of(q * quarter, 128), quarter)
@@ -374,35 +399,41 @@
 
     @pl.when(g >= 2)
     def _():
+        for h in range(2):
+            give(far, h, s_fwd, 0, core).wait_recv()
+            give(far, h, s_fwd, 0, core).start()
         res[...] += part(far)
 
     @pl.when(lax.rem(g, 2) == 1)
     def _():
-        give(core, s_fwd, 0, core).wait_recv()
+        for h in range(2):
+            give(core, h, s_fwd, 0, core).wait_recv()
         res[...] += part(core)
 
     @pl.when(g >= 2)
     def _():
-        give(3 - g, s_fwd, 0, core).wait_recv()
+        for h in range(2):
+            give(3 - g, h, s_fwd, 0, core).wait_recv()
         res[...] += part(3 - g)
 
     out[...] = res[...].astype(out.dtype)
 
-    first.wait_send()
     second.wait_send()
-    across.wait_send()
-
-    @pl.when(g < 2)
-    def _():
-        give(g, s_send, 0, far).wait_send()
-
-    @pl.when(lax.rem(g, 2) == 0)
-    def _():
-        give(g, s_send, 1, core).wait_send()
-
-    @pl.when(g >= 2)
-    def _():
-        give(far, s_fwd, 0, core).wait_send()
+    for h in range(2):
+        first[h].wait_send()
+        across[h].wait_send()
+
+        @pl.when(g < 2)
+        def _():
+            give(g, h, s_send, 0, far).wait_send()
+
+        @pl.when(lax.rem(g, 2) == 0)
+        def _():
+            give(g, h, s_send, 1, core).wait_send()
+
+        @pl.when(g >= 2)
+        def _():
+            give(far, h, s_fwd, 0, core).wait_send()
 
     def drain(e, carry):
         cp, cj = carry
@@ -458,19 +489,19 @@
                 pltpu.VMEM((total // 4, wc), BF16),
                 pltpu.VMEM((4, total // 4, wc), BF16),
                 dma((6,)),
-                dma((2 * nz, nz)),
-                dma((2 * nz, nz)),
-                dma((2 * nz, nz)),
-                dma((2 * nz, nz)),
+                dma((2 * nz, nz + 1)),
+                dma((2 * nz, nz + 1)),
+                dma((2 * nz, nz + 1)),
+                dma((2 * nz, nz + 1)),
                 dma((nz,)),
                 dma((nz,)),
+                dma((3,)),
+                dma((3,)),
                 dma((2,)),
                 dma((2,)),
-                dma,
-                dma,
-                dma((2,)),
-                dma((1,)),
-                dma((4,)),
+                dma((2, 2)),
+                dma((1, 2)),
+                dma((4, 2)),
             ],
             compiler_params=pltpu.CompilerParams(
                 collective_id=0, has_side_effects=True, vmem_limit_bytes=60 * 2**20

time: 71.2 us -> 67.4 us (0.947)
  Pallas kernels: 69.5 us -> 65.7 us
    pallas_call x1, Pallas kernels: 69.5 us -> 65.7 us  [run(): pl.pallas_call(functools.partial(panel_kernel, nz), out_shape=jax.ShapeDt...]
where the time goes in v3:
time: 67.4 us; the launch traced here: 67.3 us
  Pallas kernels  65.7 us (97%)
  local copies, waits for them, and re-layouts  1.57 us (2%)
    pallas_call x1, Pallas kernels, run(): pl.pallas_call(functools.partial(panel_kernel, nz), out_shape=jax.ShapeDt...  65.7 us
    unnamed x1, local copies, waits for them, and re-layouts  1.57 us

profile of v3, /device:TPU:29, one launch (start us, length us, event | category | flops | bytes accessed | tf_op | source)
XLA Modules:
  0.0 67.3 jit_solution(4413363307379203190)
XLA Ops:
  0.0 65.7 %shard_map.73 = bf16[256,256]{1,0:T(8,128)(2,1)} custom-call(bf16[1,192,1536]{2,1,0:T(8,128)(2,1)} %f_in.1, bf16[1,1536,256]{2,1,0:T(8,128)(2,1)} %bw_in.1, bf16[1,1536,512]{2,1,0:T(8,128)(2,1)} %bp_in.1, s32[1,2]{1,0:T(1,128)} %pat.1, bf16[1024,256]{1,0:T(8,128)(2,1)} %er_in.1, bf16[1024,1024]{1,0:T(8,128)(2,1)} %ep_in.1, bf16[256,1024]{1,0:T(8,128)(2,1)} %pv_in.1), custom_call_target="tpu_custom_call" | custom-call | tf_op jit(solution)/shard_map/pallas_call | solution.py:470
  65.7 1.6 %copy.9 = bf16[256,256]{1,0:T(8,128)(2,1)} copy(bf16[256,256]{1,0:T(8,128)(2,1)} %shard_map.73) | data formatting | bytes 262144
